TPU v7x, 512 devices: a whole 4x8x8 slice. The times are simulated.
512 devices in a mesh: dp: 2 (over core), seq: 64 (over y, z), tensor: 4 (over x).
Axes of the slice: x: 4, y: 8, z: 8, core: 2. Of those that a mesh axis runs over, the one named last changes fastest.
Arguments:
- query: bfloat16 [2, 16384, 2048], P('dp', 'seq', 'tensor'), may hold values from -1.75 to 1.75
- key_rows: bfloat16 [2, 16384, 2048], P('dp', 'seq', 'tensor'), may hold values from -1.75 to 1.75
- value: bfloat16 [2, 16384, 2048], P('dp', 'seq', 'tensor'), may hold values from -40 to 40
- gain: float32 [2048], P('tensor'), may hold values from 0.25 to 1.75
- grad_out: bfloat16 [2, 16384, 2048], P('dp', 'seq', 'tensor'), may hold values from -16 to 16
- start_offset: int32 [2, 256], P('dp', 'seq'), may hold values from 0 to 64, as said below
Outputs:
- attn_out: bfloat16 [2, 16384, 2048], P('dp', 'seq', 'tensor')
- grad_query: bfloat16 [2, 16384, 2048], P('dp', 'seq', 'tensor')
- grad_key: bfloat16 [2, 16384, 2048], P('dp', 'seq', 'tensor')
- grad_value: bfloat16 [2, 16384, 2048], P('dp', 'seq', 'tensor')
- grad_gain: float32 [2048], P('tensor')
Inputs may be any that keep to these rules, and one draw needn't show every extreme that they name: `start_offset`: the position within its block of 64 positions at which a document starts; 64 when none starts in the block; every sequence begins a document at its first position.
All inputs are finite; a program needn't handle non-finite values.
Results may differ from a plain program's by a relative error of at most 0.0058.
Values sent between devices are 32-bit elements; how exact they have to be, the bound alone decides.
No kernel may reach another device: no remote copies, remote signals or barrier semaphores. Data moves between devices by JAX's collectives and lax.ppermute only.
A program may use at most 64 MiB of HBM per device.

v0:
```python
import jax
import jax.numpy as jnp
from jax import lax
from jax.sharding import PartitionSpec as P

DH = 128
BLK = 64
CH = 2048
eps_value = 1e-05


def carried_in(part, axis, combine, identity, reverse):
    count = lax.axis_size(axis)
    place = lax.axis_index(axis)
    ahead = count - 1 - place if reverse else place
    gathered = jax.tree.map(lambda a: lax.all_gather(a, axis), part)
    state = jax.tree.map(lambda a, e: jnp.zeros_like(a) + jnp.asarray(e, a.dtype), part, identity)

    def one(turn, state):
        source = count - 1 - turn if reverse else turn
        return combine(
            state, jax.tree.map(lambda a: lax.dynamic_index_in_dim(a, source, 0, False), gathered)
        )

    return lax.fori_loop(0, ahead, one, state)


def segment_rows(offsets, length_dev):
    positions = jnp.arange(length_dev, dtype=jnp.int32)
    block_starts = jnp.arange(offsets.shape[0], dtype=jnp.int32) * BLK + offsets
    present = offsets < BLK
    covered = (block_starts[None, :] <= positions[:, None]) & present[None, :]
    labels = jnp.sum(covered.astype(jnp.int32), axis=1)
    allowed = (labels[:, None] == labels[None, :]) & (positions[None, :] <= positions[:, None])
    starts = jnp.sum(present.astype(jnp.int32))
    return (labels, starts, allowed)


def joined(earlier, later):
    return (
        jnp.where(later[1] > 0, later[0], earlier[0] + later[0]),
        jnp.maximum(earlier[1], later[1]),
    )


def shards(query, key_rows, value, gain, grad_out, start_offset):
    length_dev = query.shape[1]
    width_local = query.shape[2]
    heads_local = width_local // DH
    query_heads = query[0].reshape(length_dev, heads_local, DH)
    key_heads = key_rows[0].reshape(length_dev, heads_local, DH)
    value_heads = value[0].reshape(length_dev, heads_local, DH)
    labels, starts, allowed = segment_rows(start_offset[0], length_dev)
    head_mask = (labels == 0)[:, None, None]
    tail_mask = (labels == starts)[:, None, None]
    reset = (starts > 0).astype(jnp.int32)
    scores = jnp.einsum("thd,shd->hts", query_heads, key_heads, preferred_element_type=jnp.float32)
    weights = jnp.where(allowed[None], scores, 0.0).astype(jnp.bfloat16)
    local_out = jnp.einsum("hts,shd->thd", weights, value_heads, preferred_element_type=jnp.float32)
    tail_keys = jnp.where(tail_mask, key_heads, jnp.zeros_like(key_heads))
    tail_values = jnp.where(tail_mask, value_heads, jnp.zeros_like(value_heads))
    tail_state = jnp.einsum(
        "shi,shj->hij", tail_keys, value_heads, preferred_element_type=jnp.float32
    )
    zero_state = jnp.zeros_like(tail_state)
    incoming = carried_in((tail_state, reset), "seq", joined, (zero_state, jnp.int32(0)), False)[0]
    carried = incoming.astype(jnp.bfloat16)
    head_query = jnp.where(head_mask, query_heads, jnp.zeros_like(query_heads))
    carried_out = jnp.einsum(
        "thi,hij->thj", head_query, carried, preferred_element_type=jnp.float32
    )
    attended = (local_out + carried_out).reshape(length_dev, width_local)
    upstream = grad_out[0].astype(jnp.float32)
    scaled = gain[None, :] * upstream
    square_local = jnp.sum(attended * attended, axis=1)
    square_total = lax.psum(square_local, "tensor")
    inverse = lax.rsqrt(square_total / CH + eps_value)
    normed = attended * inverse[:, None]
    product_total = lax.psum(jnp.sum(scaled * normed, axis=1), "tensor")
    output = (gain[None, :] * normed).astype(jnp.bfloat16)
    grad_pre = (inverse[:, None] * (scaled - normed * (product_total / CH)[:, None])).astype(
        jnp.bfloat16
    )
    gain_local = jnp.sum(upstream * normed, axis=0)
    grad_gain = lax.psum(gain_local, ("dp", "seq"))
    grad_heads = grad_pre.reshape(length_dev, heads_local, DH)
    grad_state = jnp.einsum(
        "thi,thj->hij", head_query, grad_heads, preferred_element_type=jnp.float32
    )
    later = carried_in((grad_state, reset), "seq", joined, (zero_state, jnp.int32(0)), True)[0]
    later_half = later.astype(jnp.bfloat16)
    grad_scores = jnp.einsum(
        "thd,shd->hts", grad_heads, value_heads, preferred_element_type=jnp.float32
    )
    grad_weights = jnp.where(allowed[None], grad_scores, 0.0).astype(jnp.bfloat16)
    head_grad = jnp.where(head_mask, grad_heads, jnp.zeros_like(grad_heads))
    grad_query = jnp.einsum(
        "hts,shd->thd", grad_weights, key_heads, preferred_element_type=jnp.float32
    ) + jnp.einsum("thj,hij->thi", head_grad, carried, preferred_element_type=jnp.float32)
    grad_key = jnp.einsum(
        "hts,thd->shd", grad_weights, query_heads, preferred_element_type=jnp.float32
    ) + jnp.einsum("shj,hij->shi", tail_values, later_half, preferred_element_type=jnp.float32)
    grad_value = jnp.einsum(
        "hts,thd->shd", weights, grad_heads, preferred_element_type=jnp.float32
    ) + jnp.einsum("shi,hij->shj", tail_keys, later_half, preferred_element_type=jnp.float32)
    shape_dev = (1, length_dev, width_local)
    return (
        output.reshape(shape_dev),
        grad_query.reshape(shape_dev).astype(jnp.bfloat16),
        grad_key.reshape(shape_dev).astype(jnp.bfloat16),
        grad_value.reshape(shape_dev).astype(jnp.bfloat16),
        grad_gain,
    )


def solution(mesh):
    return jax.shard_map(
        shards,
        mesh=mesh,
        in_specs=(
            P("dp", "seq", "tensor"),
            P("dp", "seq", "tensor"),
            P("dp", "seq", "tensor"),
            P("tensor"),
            P("dp", "seq", "tensor"),
            P("dp", "seq"),
        ),
        out_specs=(
            P("dp", "seq", "tensor"),
            P("dp", "seq", "tensor"),
            P("dp", "seq", "tensor"),
            P("dp", "seq", "tensor"),
            P("tensor"),
        ),
        check_vma=False,
    )
```

profile of v0, /device:TPU:1, one launch (start us, length us, event | category | flops | bytes accessed | tf_op | source)
XLA Modules:
  0.0 739.9 jit_solution(13396427716960763037)
XLA Ops:
  7.9 1.3 fusion.29
  9.2 1.1 copy.54
  10.3 1.1 copy.57
  13.8 1.1 copy.53
  14.9 1.1 copy.62
  15.9 1.3 dynamic-slice
  18.0 26.8 %all-reduce = s32[64]{0:T(128)S(1)} all-reduce(s32[64]{0:T(128)S(1)} %dynamic-update-slice), channel_id=1, replica_groups=mesh['dp'=2,'seq'=64,'tensor'=4] {'seq'}, use_global_device_ids=true, to_apply=%add | all-reduce | flops 64 | bytes 512
  45.6 112.6 %all-gather.5.cloned.1.call-done = f32[256,128,128]{2,1,0:T(8,128)} async-done(((f32[4,128,128]{2,1,0:T(8,128)}), f32[256,128,128]{2,1,0:T(8,128)}) %all-gather.5.cloned.1.call-update) | async-done | bytes 16777232 | tf_op jit(solution)/shard_map/all_gather | solution.py:16
  158.5 8.4 %psum.21 = f32[256]{0:T(256)S(1)} all-reduce(f32[256]{0:T(256)S(1)} %get-tuple-element.176), channel_id=1, replica_groups=mesh['dp'=2,'seq'=64,'tensor'=4] {'tensor'}, use_global_device_ids=true, to_apply=%region_5.6 | all-reduce | flops 256 | bytes 2048 | tf_op jit(solution)/shard_map/psum | solution.py:76
  167.1 1.2 fusion.10
  168.3 6.0 psum.22
  178.1 405.6 %psum.23 = f32[512]{0:T(512)} all-reduce(f32[512]{0:T(512)S(1)} %get-tuple-element.150), channel_id=1, replica_groups=mesh['dp'=2,'seq'=64,'tensor'=4] {'dp','seq'}, use_global_device_ids=true, to_apply=%region_11.12 | all-reduce | flops 512 | bytes 4096 | tf_op jit(solution)/shard_map/psum | solution.py:85
  585.0 145.9 %while.27 = (s32[]{:T(128)}, f32[4,128,128]{2,1,0:T(8,128)S(1)}, s32[]{:T(128)}, s32[64]{0:T(128)S(1)}, f32[64,4,128,128]{3,2,1,0:T(8,128)}, /*index=5*/s32[]{:T(128)}, s32[]{:T(128)}, s32[]{:T(128)}, s32[]{:T(128)}, s32[1]{0:T(128)}) while((s32[]{:T(128)}, f32[4,128,128]{2,1,0:T(8,128)S(1)}, s32[]{:T(128)}, s32[64]{0:T(128)S(1)}, ...), condition=%wide.region_9.10_spmd, body=%wide.region_8.9_spmd.sunk | while | flops 131079 | bytes 786613 | solution.py:25
  586.3 1.1 add_select_fusion.5
  588.6 1.1 add_select_fusion.5
  590.9 1.1 add_select_fusion.5
  595.5 1.1 add_select_fusion.5
  600.2 1.1 add_select_fusion.5
  604.8 1.1 add_select_fusion.5
  609.4 1.1 add_select_fusion.5
  614.1 1.1 add_select_fusion.5
  618.7 1.1 add_select_fusion.5
  623.3 1.1 add_select_fusion.5
  625.7 1.1 add_select_fusion.5
  628.0 1.1 add_select_fusion.5
  630.3 1.1 add_select_fusion.5
  632.6 1.1 add_select_fusion.5
  634.9 1.1 add_select_fusion.5
  639.5 1.1 add_select_fusion.5
  644.2 1.1 add_select_fusion.5
  648.8 1.1 add_select_fusion.5
  653.4 1.1 add_select_fusion.5
  (144 shorter events, 95.0 us)
Async XLA Ops:
  7.2 576.5 %copy-start = (f32[512]{0:T(512)S(1)}, f32[512]{0:T(512)}, u32[]{:S(2)}) copy-start(f32[512]{0:T(512)} %param.13) | copy-start | bytes 6148
  7.2 151.0 %all-gather.5.cloned.1.call-start = ((), (), s32[]{:S(2)}) async-start(), calls=%async_computation | async-start | bytes 17039360 | tf_op jit(solution)/shard_map/all_gather | solution.py:16
  13.1 571.9 %all-gather.7.cloned.1.call-start = ((), (), s32[]{:S(2)}) async-start(), calls=%async_computation.1 | async-start | bytes 17039360 | tf_op jit(solution)/shard_map/all_gather | solution.py:16
Sparse Core Ops, SparseCore 0:
  13.2 144.9 all-gather.4
  176.2 284.0 all-gather.6
where the time goes:
time: 743 us; the launch traced here: 740 us
  blocking collectives  447 us (60%)
  waiting for transfers between devices  113 us (15%)
  other arithmetic  71.9 us (10%)
  local copies, waits for them, and re-layouts  46.4 us (6%)
  loops' own time  42.6 us (6%)
  between operations  14.9 us (2%)
    psum x1, blocking collectives, shards(): grad_gain = lax.psum(gain_local, ('dp', 'seq'))  406 us
    all_gather x2, waiting for transfers between devices, carried_in(): gathered = jax.tree.map(lambda a: lax.all_gather(a, axis), part)  113 us
    select_n x63, other arithmetic, joined(): jnp.where(later[1] > 0, later[0], earlier[0] + later[0])  66.2 us
    another operation x2, loops' own time, carried_in(): return lax.fori_loop(0, ahead, one, state)  42.6 us
    dynamic_slice x63, local copies, waits for them, and re-layouts, one(): lax.dynamic_index_in_dim(a, source, 0, False)  37.1 us
    unnamed x1, blocking collectives  26.8 us
  transfers between devices with their start and end apart: 2, of which 1 were waited for; matrix products, arithmetic and copies ran while one was open for 1% of the time, Pallas kernels for 0%

commit v1 on v0

--- a/solution.py
+++ b/solution.py
@@ -82,7 +82,8 @@
         jnp.bfloat16
     )
     gain_local = jnp.sum(upstream * normed, axis=0)
-    grad_gain = lax.psum(gain_local, ("dp", "seq"))
+    inner = lax.psum(gain_local, "dp")
+    grad_gain = lax.psum(inner, "seq")
     grad_heads = grad_pre.reshape(length_dev, heads_local, DH)
     grad_state = jnp.einsum(
         "thi,thj->hij", head_query, grad_heads, preferred_element_type=jnp.float32

time: 743 us -> 636 us (0.86)
  the two profiles are of different devices: /device:TPU:1 before, /device:TPU:2 now
where the time goes in v1:
time: 636 us; the launch traced here: 633 us
  blocking collectives  344 us (54%)
  waiting for transfers between devices  108 us (17%)
  other arithmetic  71.9 us (11%)
  local copies, waits for them, and re-layouts  46.4 us (7%)
  loops' own time  42.6 us (7%)
  between operations  14.9 us (2%)
    psum x1, blocking collectives, shards(): grad_gain = lax.psum(inner, 'seq')  292 us
    all_gather x2, waiting for transfers between devices, carried_in(): gathered = jax.tree.map(lambda a: lax.all_gather(a, axis), part)  108 us
    select_n x63, other arithmetic, joined(): jnp.where(later[1] > 0, later[0], earlier[0] + later[0])  66.2 us
    another operation x2, loops' own time, carried_in(): return lax.fori_loop(0, ahead, one, state)  42.6 us
    dynamic_slice x63, local copies, waits for them, and re-layouts, one(): lax.dynamic_index_in_dim(a, source, 0, False)  37.1 us
    unnamed x1, blocking collectives  31 us
  transfers between devices with their start and end apart: 2, of which 1 were waited for; matrix products, arithmetic and copies ran while one was open for 1% of the time, Pallas kernels for 0%

profile of v1, /device:TPU:2, one launch (start us, length us, event | category | flops | bytes accessed | tf_op | source)
XLA Modules:
  0.0 632.5 jit_solution(12725390414444873696)
XLA Ops:
  7.9 1.3 fusion.29
  9.2 1.1 copy.54
  10.3 1.1 copy.57
  13.8 1.1 copy.53
  14.9 1.1 copy.62
  15.9 1.3 dynamic-slice
  18.0 31.0 %all-reduce = s32[64]{0:T(128)S(1)} all-reduce(s32[64]{0:T(128)S(1)} %dynamic-update-slice), channel_id=1, replica_groups=mesh['dp'=2,'seq'=64,'tensor'=4] {'seq'}, use_global_device_ids=true, to_apply=%add | all-reduce | flops 64 | bytes 512
  49.8 107.7 %all-gather.5.cloned.1.call-done = f32[256,128,128]{2,1,0:T(8,128)} async-done(((f32[4,128,128]{2,1,0:T(8,128)}), f32[256,128,128]{2,1,0:T(8,128)}) %all-gather.5.cloned.1.call-update) | async-done | bytes 16777232 | tf_op jit(solution)/shard_map/all_gather | solution.py:16
  157.8 8.6 %psum.28 = f32[256]{0:T(256)S(1)} all-reduce(f32[256]{0:T(256)S(1)} %get-tuple-element.176), channel_id=1, replica_groups=mesh['dp'=2,'seq'=64,'tensor'=4] {'tensor'}, use_global_device_ids=true, to_apply=%region_5.6 | all-reduce | flops 256 | bytes 2048 | tf_op jit(solution)/shard_map/psum | solution.py:76
  166.6 1.2 fusion.10
  167.8 10.1 %psum.29 = f32[256]{0:T(256)S(1)} all-reduce(f32[256]{0:T(256)S(1)} %get-tuple-element.151), channel_id=1, replica_groups=mesh['dp'=2,'seq'=64,'tensor'=4] {'tensor'}, use_global_device_ids=true, to_apply=%region_7.8 | all-reduce | flops 256 | bytes 2048 | tf_op jit(solution)/shard_map/psum | solution.py:79
  181.7 2.4 psum.30
  184.1 292.2 %psum.31 = f32[512]{0:T(512)} all-reduce(f32[512]{0:T(512)S(1)} %psum.30), channel_id=1, replica_groups=mesh['dp'=2,'seq'=64,'tensor'=4] {'seq'}, use_global_device_ids=true, to_apply=%region_12.13 | all-reduce | flops 512 | bytes 4096 | tf_op jit(solution)/shard_map/psum | solution.py:86
  477.6 145.9 %while.27 = (s32[]{:T(128)}, f32[4,128,128]{2,1,0:T(8,128)S(1)}, s32[]{:T(128)}, s32[64]{0:T(128)S(1)}, f32[64,4,128,128]{3,2,1,0:T(8,128)}, /*index=5*/s32[]{:T(128)}, s32[]{:T(128)}, s32[]{:T(128)}, s32[]{:T(128)}, s32[1]{0:T(128)}) while((s32[]{:T(128)}, f32[4,128,128]{2,1,0:T(8,128)S(1)}, s32[]{:T(128)}, s32[64]{0:T(128)S(1)}, ...), condition=%wide.region_9.10_spmd, body=%wide.region_8.9_spmd.sunk | while | flops 131079 | bytes 786613 | solution.py:25
  481.2 1.1 add_select_fusion.5
  483.5 1.1 add_select_fusion.5
  485.8 1.1 add_select_fusion.5
  488.1 1.1 add_select_fusion.5
  490.5 1.1 add_select_fusion.5
  492.8 1.1 add_select_fusion.5
  497.4 1.1 add_select_fusion.5
  502.0 1.1 add_select_fusion.5
  506.7 1.1 add_select_fusion.5
  511.3 1.1 add_select_fusion.5
  515.9 1.1 add_select_fusion.5
  520.6 1.1 add_select_fusion.5
  525.2 1.1 add_select_fusion.5
  527.5 1.1 add_select_fusion.5
  529.8 1.1 add_select_fusion.5
  532.1 1.1 add_select_fusion.5
  534.5 1.1 add_select_fusion.5
  536.8 1.1 add_select_fusion.5
  (145 shorter events, 96.1 us)
Async XLA Ops:
  7.2 469.1 %copy-start = (f32[512]{0:T(512)S(1)}, f32[512]{0:T(512)}, u32[]{:S(2)}) copy-start(f32[512]{0:T(512)} %param.13) | copy-start | bytes 6148
  7.2 150.3 %all-gather.5.cloned.1.call-start = ((), (), s32[]{:S(2)}) async-start(), calls=%async_computation | async-start | bytes 17039360 | tf_op jit(solution)/shard_map/all_gather | solution.py:16
  13.1 464.5 %all-gather.7.cloned.1.call-start = ((), (), s32[]{:S(2)}) async-start(), calls=%async_computation.1 | async-start | bytes 17039360 | tf_op jit(solution)/shard_map/all_gather | solution.py:16
Sparse Core Ops, SparseCore 0:
  13.2 144.2 all-gather.4
  179.9 279.6 all-gather.6
